TPU v7x, 512 devices: a whole 4x4x16 slice. The times are simulated.
512 devices in a mesh: row: 16 (over x, y), col: 32 (over z, core).
Axes of the slice: x: 4, y: 4, z: 16, core: 2. Of those that a mesh axis runs over, the one named last changes fastest.
Arguments:
- positions: float32 [3, 32768], P(None, ('row', 'col')), may hold values from -1 to 96, as said below
- noise: float32 [8, 3, 32768], P(None, None, ('row', 'col')), may hold values from -6 to 6
Outputs:
- basis: float32 [8, 3, 32768], P(None, None, ('row', 'col'))
- residual: float32 [8, 3, 32768], P(None, None, ('row', 'col'))
- coefficients: float32 [3, 8, 8], replicated
Inputs may be any that keep to these rules, and one draw needn't show every extreme that they name: `positions`: bead k lies within 0.77 of each coordinate of its own point of a cubic lattice of spacing 2.2 with 32 by 32 points a layer, distinct beads on distinct points.
All inputs are finite; a program needn't handle non-finite values.
Results may differ from a plain program's by a relative error of at most 0.0003.
Values sent between devices are 32-bit elements; how exact they have to be, the bound alone decides.
A program may use at most 64 MiB of HBM per device.

v0:
```python
import jax
import jax.numpy as jnp
from jax import lax
from jax.sharding import PartitionSpec as P


def pair_tensor(target_pos, source_pos):
    displace = target_pos[:, :, None] - source_pos[:, None, :]
    distance_sq = jnp.sum(displace * displace, axis=0)
    distance = jnp.sqrt(distance_sq)
    safe_distance = jnp.where(distance > 0, distance, 1.0)
    safe_sq = safe_distance * safe_distance
    far_iso = 0.75 / safe_distance * (1.0 + 2.0 / (3.0 * safe_sq))
    far_dir = 0.75 / safe_distance * (1.0 - 2.0 / safe_sq) / safe_sq
    near_iso = 1.0 - 9.0 * distance / 32.0
    near_dir = 3.0 / (32.0 * safe_distance)
    intersecting = distance < 2.0
    iso_part = jnp.where(intersecting, near_iso, far_iso)
    dir_part = jnp.where(intersecting, near_dir, far_dir)
    identity = jnp.eye(3, dtype=displace.dtype)
    return identity[:, :, None, None] * iso_part + dir_part * displace[:, None] * displace[None, :]


def local_gram(left, right):
    return jnp.einsum("kan,jan->kj", left, right, precision=lax.Precision.HIGHEST)


def combine(vectors, matrix):
    return jnp.einsum("kan,kj->jan", vectors, matrix, precision=lax.Precision.HIGHEST)


def lower_inverse(factor):
    return jax.scipy.linalg.solve_triangular(
        factor, jnp.eye(factor.shape[0], dtype=factor.dtype), lower=True
    )


def local(positions, noise):
    local_beads = positions.shape[1]
    total_count = 3.0 * local_beads * lax.axis_size("row") * lax.axis_size("col")
    target_pos = lax.all_gather(positions, "row", axis=1, tiled=True)
    source_pos = lax.all_gather(positions, "col", axis=1, tiled=True)

    def mobility(vectors):
        initial = jnp.zeros((vectors.shape[0], 3, target_pos.shape[1]), jnp.float32)
        source_piece = lax.all_gather(vectors, "col", axis=2, tiled=True)
        piece_width = source_piece.shape[2]
        block_count = 1
        while piece_width % block_count != 0 or piece_width // block_count > 256:
            block_count = block_count + 1
        block_width = piece_width // block_count

        def add_block(block_index, running):
            block_pos = lax.dynamic_slice_in_dim(
                source_pos, block_index * block_width, block_width, 1
            )
            block_vectors = lax.dynamic_slice_in_dim(
                source_piece, block_index * block_width, block_width, 2
            )
            tensor = pair_tensor(target_pos, block_pos)
            return running + jnp.einsum(
                "abts,kbs->kat", tensor, block_vectors, precision=lax.Precision.HIGHEST
            )

        partial_image = lax.fori_loop(0, block_count, add_block, initial)
        summed = lax.psum(partial_image, "row")
        return lax.dynamic_slice_in_dim(summed, lax.axis_index("row") * local_beads, local_beads, 2)

    start_matrix = lax.psum(local_gram(noise, noise), ("row", "col")) / total_count
    start_factor = jnp.linalg.cholesky(start_matrix)
    first = combine(noise, lower_inverse(start_factor).T)
    image = mobility(first)
    alpha_one = lax.psum(local_gram(first, image), ("row", "col")) / total_count
    remainder = image - combine(first, alpha_one)
    residual_matrix = lax.psum(local_gram(remainder, remainder), ("row", "col")) / total_count
    factor_one = jnp.linalg.cholesky(residual_matrix)
    basis = combine(remainder, lower_inverse(factor_one).T)
    image = mobility(basis) - combine(first, factor_one)
    alpha_two = lax.psum(local_gram(basis, image), ("row", "col")) / total_count
    residual = image - combine(basis, alpha_two)
    return (basis, residual, jnp.stack([alpha_one, factor_one, alpha_two]))


def solution(mesh):
    return jax.shard_map(
        local,
        mesh=mesh,
        in_specs=(P(None, ("row", "col")), P(None, None, ("row", "col"))),
        out_specs=(P(None, None, ("row", "col")), P(None, None, ("row", "col")), P()),
        check_vma=False,
    )
```

profile of v0, /device:TPU:1, one launch (start us, length us, event | category | flops | bytes accessed | tf_op | source)
XLA Modules:
  0.0 1041.4 jit_solution(14341036072423276544)
XLA Ops:
  7.2 38.0 %all-gather.1 = f32[32,64,3]{1,2,0:T(4,128)S(1)} all-gather(f32[1,64,3]{1,2,0:T(4,128)} %bitcast.96), channel_id=1, replica_groups=mesh['row'=16,'col'=32] {'col'}, dimensions={0}, use_global_device_ids=true | all-gather | bytes 25344 | tf_op jit(solution)/shard_map/all_gather | solution.py:42
  45.2 18.3 %all-gather = f32[16,64,3]{1,2,0:T(4,128)S(1)} all-gather(f32[1,64,3]{1,2,0:T(4,128)} %bitcast.97), channel_id=1, replica_groups=mesh['row'=16,'col'=32] {'row'}, dimensions={0}, use_global_device_ids=true | all-gather | bytes 13056 | tf_op jit(solution)/shard_map/all_gather | solution.py:41
  63.7 104.2 %psum.42 = f32[8,8]{0,1:T(8,128)S(1)} all-reduce(f32[8,8]{0,1:T(8,128)S(1)} %convolution_bitcast_fusion.5), channel_id=1, replica_groups=mesh['row'=16,'col'=32] {'row','col'}, use_global_device_ids=true, to_apply=%region_0.0 | all-reduce | flops 64 | bytes 512 | tf_op jit(solution)/shard_map/psum | solution.py:69
  171.1 44.3 %all_gather.12 = f32[8,3,2048]{0,1,2:T(4,128)} all-gather(f32[8,3,64]{0,1,2:T(4,128)S(1)} %copy.36), channel_id=1, replica_groups=mesh['row'=16,'col'=32] {'col'}, dimensions={2}, use_global_device_ids=true | all-gather | bytes 202752 | tf_op jit(solution)/shard_map/all_gather | solution.py:46
  215.4 3.3 copy.39
  218.9 120.9 %while.32 = (s32[]{:T(128)}, f32[8,3,1024]{2,0,1:T(8,128)S(1)}, f32[8,3,2048]{2,0,1:T(8,128)S(1)}, f32[3,1024]{1,0:T(4,128)S(1)}, f32[3,2048]{1,0:T(4,128)S(1)},...) while((s32[]{:T(128)}, f32[8,3,1024]{2,0,1:T(8,128)S(1)}, f32[8,3,2048]{2,0,1:T(8,128)S(1)}, ...), condition=%wide.region_5.8_spmd.clone, body=%wide.region_3.7_spmd.clone.sunk | while | flops 242270240 | bytes 19134656 | solution.py:65
  219.4 2.0 multiply_select_fusion.4
  221.4 2.1 subtract_multiply_fusion.4
  223.5 10.5 %fusion.87 = f32[8,3,1024]{2,0,1:T(8,128)S(1)} fusion(f32[3,1024,256]{2,1,0:T(8,128)} %get-tuple-element.423, f32[3,1024,256]{2,1,0:T(8,128)S(1)} %get-tuple-element.424, f32[1024,256]{1,0:T(8,128)} %get-tuple-element.425, f32[3,3]{1,0:T(4,128)S(1)} %fusion.86, f32[8,3,1024]{2,0,1:T(8,128)S(1)} %get-tuple-element.445, pred[]{:T(512)S(6)} %compare.14, ...), kind=kOutput, calls=%fused_computation.13.clone.1 | convolution fusion | flops 233619456 | bytes 7563269 | tf_op jit(solution)/shard_map/while/body/eval_jaxpr/abts,kbs->kat/dot_general | solution.py:61
  234.5 2.0 multiply_select_fusion.4
  236.5 2.1 subtract_multiply_fusion.4
  238.7 10.5 %fusion.87 = f32[8,3,1024]{2,0,1:T(8,128)S(1)} fusion(f32[3,1024,256]{2,1,0:T(8,128)} %get-tuple-element.423, f32[3,1024,256]{2,1,0:T(8,128)S(1)} %get-tuple-element.424, f32[1024,256]{1,0:T(8,128)} %get-tuple-element.425, f32[3,3]{1,0:T(4,128)S(1)} %fusion.86, f32[8,3,1024]{2,0,1:T(8,128)S(1)} %get-tuple-element.445, pred[]{:T(512)S(6)} %compare.14, ...), kind=kOutput, calls=%fused_computation.13.clone.1 | convolution fusion | flops 233619456 | bytes 7563269 | tf_op jit(solution)/shard_map/while/body/eval_jaxpr/abts,kbs->kat/dot_general | solution.py:61
  249.6 2.0 multiply_select_fusion.4
  251.6 2.1 subtract_multiply_fusion.4
  253.8 10.5 %fusion.87 = f32[8,3,1024]{2,0,1:T(8,128)S(1)} fusion(f32[3,1024,256]{2,1,0:T(8,128)} %get-tuple-element.423, f32[3,1024,256]{2,1,0:T(8,128)S(1)} %get-tuple-element.424, f32[1024,256]{1,0:T(8,128)} %get-tuple-element.425, f32[3,3]{1,0:T(4,128)S(1)} %fusion.86, f32[8,3,1024]{2,0,1:T(8,128)S(1)} %get-tuple-element.445, pred[]{:T(512)S(6)} %compare.14, ...), kind=kOutput, calls=%fused_computation.13.clone.1 | convolution fusion | flops 233619456 | bytes 7563269 | tf_op jit(solution)/shard_map/while/body/eval_jaxpr/abts,kbs->kat/dot_general | solution.py:61
  264.8 2.0 multiply_select_fusion.4
  266.8 2.1 subtract_multiply_fusion.4
  268.9 10.5 %fusion.87 = f32[8,3,1024]{2,0,1:T(8,128)S(1)} fusion(f32[3,1024,256]{2,1,0:T(8,128)} %get-tuple-element.423, f32[3,1024,256]{2,1,0:T(8,128)S(1)} %get-tuple-element.424, f32[1024,256]{1,0:T(8,128)} %get-tuple-element.425, f32[3,3]{1,0:T(4,128)S(1)} %fusion.86, f32[8,3,1024]{2,0,1:T(8,128)S(1)} %get-tuple-element.445, pred[]{:T(512)S(6)} %compare.14, ...), kind=kOutput, calls=%fused_computation.13.clone.1 | convolution fusion | flops 233619456 | bytes 7563269 | tf_op jit(solution)/shard_map/while/body/eval_jaxpr/abts,kbs->kat/dot_general | solution.py:61
  279.9 2.0 multiply_select_fusion.4
  281.9 2.1 subtract_multiply_fusion.4
  284.0 10.5 %fusion.87 = f32[8,3,1024]{2,0,1:T(8,128)S(1)} fusion(f32[3,1024,256]{2,1,0:T(8,128)} %get-tuple-element.423, f32[3,1024,256]{2,1,0:T(8,128)S(1)} %get-tuple-element.424, f32[1024,256]{1,0:T(8,128)} %get-tuple-element.425, f32[3,3]{1,0:T(4,128)S(1)} %fusion.86, f32[8,3,1024]{2,0,1:T(8,128)S(1)} %get-tuple-element.445, pred[]{:T(512)S(6)} %compare.14, ...), kind=kOutput, calls=%fused_computation.13.clone.1 | convolution fusion | flops 233619456 | bytes 7563269 | tf_op jit(solution)/shard_map/while/body/eval_jaxpr/abts,kbs->kat/dot_general | solution.py:61
  295.0 2.0 multiply_select_fusion.4
  297.0 2.1 subtract_multiply_fusion.4
  299.1 10.5 %fusion.87 = f32[8,3,1024]{2,0,1:T(8,128)S(1)} fusion(f32[3,1024,256]{2,1,0:T(8,128)} %get-tuple-element.423, f32[3,1024,256]{2,1,0:T(8,128)S(1)} %get-tuple-element.424, f32[1024,256]{1,0:T(8,128)} %get-tuple-element.425, f32[3,3]{1,0:T(4,128)S(1)} %fusion.86, f32[8,3,1024]{2,0,1:T(8,128)S(1)} %get-tuple-element.445, pred[]{:T(512)S(6)} %compare.14, ...), kind=kOutput, calls=%fused_computation.13.clone.1 | convolution fusion | flops 233619456 | bytes 7563269 | tf_op jit(solution)/shard_map/while/body/eval_jaxpr/abts,kbs->kat/dot_general | solution.py:61
  310.1 2.0 multiply_select_fusion.4
  312.1 2.1 subtract_multiply_fusion.4
  314.2 10.5 %fusion.87 = f32[8,3,1024]{2,0,1:T(8,128)S(1)} fusion(f32[3,1024,256]{2,1,0:T(8,128)} %get-tuple-element.423, f32[3,1024,256]{2,1,0:T(8,128)S(1)} %get-tuple-element.424, f32[1024,256]{1,0:T(8,128)} %get-tuple-element.425, f32[3,3]{1,0:T(4,128)S(1)} %fusion.86, f32[8,3,1024]{2,0,1:T(8,128)S(1)} %get-tuple-element.445, pred[]{:T(512)S(6)} %compare.14, ...), kind=kOutput, calls=%fused_computation.13.clone.1 | convolution fusion | flops 233619456 | bytes 7563269 | tf_op jit(solution)/shard_map/while/body/eval_jaxpr/abts,kbs->kat/dot_general | solution.py:61
  325.2 2.0 multiply_select_fusion.4
  327.2 2.1 subtract_multiply_fusion.4
  329.4 10.5 %fusion.87 = f32[8,3,1024]{2,0,1:T(8,128)S(1)} fusion(f32[3,1024,256]{2,1,0:T(8,128)} %get-tuple-element.423, f32[3,1024,256]{2,1,0:T(8,128)S(1)} %get-tuple-element.424, f32[1024,256]{1,0:T(8,128)} %get-tuple-element.425, f32[3,3]{1,0:T(4,128)S(1)} %fusion.86, f32[8,3,1024]{2,0,1:T(8,128)S(1)} %get-tuple-element.445, pred[]{:T(512)S(6)} %compare.14, ...), kind=kOutput, calls=%fused_computation.13.clone.1 | convolution fusion | flops 233619456 | bytes 7563269 | tf_op jit(solution)/shard_map/while/body/eval_jaxpr/abts,kbs->kat/dot_general | solution.py:61
  340.6 103.5 %all-reduce.3.cloned.1.call-done = f32[8,3,1024]{2,0,1:T(8,128)} async-done(((f32[8,3,1024]{2,0,1:T(8,128)}), f32[8,3,1024]{2,0,1:T(8,128)}) %all-reduce.3.cloned.1.call-update) | async-done | bytes 98320 | tf_op jit(solution)/shard_map/psum | solution.py:66
  444.0 0.9 convolution_bitcast_fusion.3
  444.9 104.2 %psum.44 = f32[8,8]{0,1:T(8,128)S(1)} all-reduce(f32[8,8]{0,1:T(8,128)S(1)} %convolution_bitcast_fusion.3), channel_id=1, replica_groups=mesh['row'=16,'col'=32] {'row','col'}, use_global_device_ids=true, to_apply=%region_7.10 | all-reduce | flops 64 | bytes 512 | tf_op jit(solution)/shard_map/psum | solution.py:73
  550.1 100.2 %psum.45 = f32[8,8]{0,1:T(8,128)S(1)} all-reduce(f32[8,8]{0,1:T(8,128)S(1)} %convolution_bitcast_fusion.2), channel_id=1, replica_groups=mesh['row'=16,'col'=32] {'row','col'}, use_global_device_ids=true, to_apply=%region_8.11 | all-reduce | flops 64 | bytes 512 | tf_op jit(solution)/shard_map/psum | solution.py:75
  653.5 43.3 %all_gather.15 = f32[8,3,2048]{0,1,2:T(4,128)} all-gather(f32[8,3,64]{0,1,2:T(4,128)S(1)} %copy.44), channel_id=1, replica_groups=mesh['row'=16,'col'=32] {'col'}, dimensions={2}, use_global_device_ids=true | all-gather | bytes 202752 | tf_op jit(solution)/shard_map/all_gather | solution.py:46
  696.8 3.3 copy.45
  700.1 120.9 %while.33 = (s32[]{:T(128)}, f32[8,3,1024]{2,0,1:T(8,128)S(1)}, f32[8,3,2048]{2,0,1:T(8,128)S(1)}, f32[3,1024]{1,0:T(4,128)S(1)}, f32[3,2048]{1,0:T(4,128)S(1)},...) while((s32[]{:T(128)}, f32[8,3,1024]{2,0,1:T(8,128)S(1)}, f32[8,3,2048]{2,0,1:T(8,128)S(1)}, ...), condition=%wide.region_11.14_spmd.clone, body=%wide.region_9.13_spmd.clone.sunk | while | flops 242270240 | bytes 19134656 | solution.py:65
  700.6 2.0 multiply_select_fusion.5
  702.6 2.1 subtract_multiply_fusion.5
  704.8 10.5 %fusion.91 = f32[8,3,1024]{2,0,1:T(8,128)S(1)} fusion(f32[3,1024,256]{2,1,0:T(8,128)} %get-tuple-element.432, f32[3,1024,256]{2,1,0:T(8,128)S(1)} %get-tuple-element.433, f32[1024,256]{1,0:T(8,128)} %get-tuple-element.434, f32[3,3]{1,0:T(4,128)S(1)} %fusion.90, f32[8,3,1024]{2,0,1:T(8,128)S(1)} %get-tuple-element.472, pred[]{:T(512)S(6)} %compare.15, ...), kind=kOutput, calls=%fused_computation.37.clone.1 | convolution fusion | flops 233619456 | bytes 7563269 | tf_op jit(solution)/shard_map/while/body/eval_jaxpr/abts,kbs->kat/dot_general | solution.py:61
  715.8 2.0 multiply_select_fusion.5
  717.8 2.1 subtract_multiply_fusion.5
  719.9 10.5 %fusion.91 = f32[8,3,1024]{2,0,1:T(8,128)S(1)} fusion(f32[3,1024,256]{2,1,0:T(8,128)} %get-tuple-element.432, f32[3,1024,256]{2,1,0:T(8,128)S(1)} %get-tuple-element.433, f32[1024,256]{1,0:T(8,128)} %get-tuple-element.434, f32[3,3]{1,0:T(4,128)S(1)} %fusion.90, f32[8,3,1024]{2,0,1:T(8,128)S(1)} %get-tuple-element.472, pred[]{:T(512)S(6)} %compare.15, ...), kind=kOutput, calls=%fused_computation.37.clone.1 | convolution fusion | flops 233619456 | bytes 7563269 | tf_op jit(solution)/shard_map/while/body/eval_jaxpr/abts,kbs->kat/dot_general | solution.py:61
  730.9 2.0 multiply_select_fusion.5
  732.9 2.1 subtract_multiply_fusion.5
  735.0 10.5 %fusion.91 = f32[8,3,1024]{2,0,1:T(8,128)S(1)} fusion(f32[3,1024,256]{2,1,0:T(8,128)} %get-tuple-element.432, f32[3,1024,256]{2,1,0:T(8,128)S(1)} %get-tuple-element.433, f32[1024,256]{1,0:T(8,128)} %get-tuple-element.434, f32[3,3]{1,0:T(4,128)S(1)} %fusion.90, f32[8,3,1024]{2,0,1:T(8,128)S(1)} %get-tuple-element.472, pred[]{:T(512)S(6)} %compare.15, ...), kind=kOutput, calls=%fused_computation.37.clone.1 | convolution fusion | flops 233619456 | bytes 7563269 | tf_op jit(solution)/shard_map/while/body/eval_jaxpr/abts,kbs->kat/dot_general | solution.py:61
  746.0 2.0 multiply_select_fusion.5
  748.0 2.1 subtract_multiply_fusion.5
  750.1 10.5 %fusion.91 = f32[8,3,1024]{2,0,1:T(8,128)S(1)} fusion(f32[3,1024,256]{2,1,0:T(8,128)} %get-tuple-element.432, f32[3,1024,256]{2,1,0:T(8,128)S(1)} %get-tuple-element.433, f32[1024,256]{1,0:T(8,128)} %get-tuple-element.434, f32[3,3]{1,0:T(4,128)S(1)} %fusion.90, f32[8,3,1024]{2,0,1:T(8,128)S(1)} %get-tuple-element.472, pred[]{:T(512)S(6)} %compare.15, ...), kind=kOutput, calls=%fused_computation.37.clone.1 | convolution fusion | flops 233619456 | bytes 7563269 | tf_op jit(solution)/shard_map/while/body/eval_jaxpr/abts,kbs->kat/dot_general | solution.py:61
  761.1 2.0 multiply_select_fusion.5
  763.1 2.1 subtract_multiply_fusion.5
  765.2 10.5 %fusion.91 = f32[8,3,1024]{2,0,1:T(8,128)S(1)} fusion(f32[3,1024,256]{2,1,0:T(8,128)} %get-tuple-element.432, f32[3,1024,256]{2,1,0:T(8,128)S(1)} %get-tuple-element.433, f32[1024,256]{1,0:T(8,128)} %get-tuple-element.434, f32[3,3]{1,0:T(4,128)S(1)} %fusion.90, f32[8,3,1024]{2,0,1:T(8,128)S(1)} %get-tuple-element.472, pred[]{:T(512)S(6)} %compare.15, ...), kind=kOutput, calls=%fused_computation.37.clone.1 | convolution fusion | flops 233619456 | bytes 7563269 | tf_op jit(solution)/shard_map/while/body/eval_jaxpr/abts,kbs->kat/dot_general | solution.py:61
  776.2 2.0 multiply_select_fusion.5
  778.2 2.1 subtract_multiply_fusion.5
  780.4 10.5 %fusion.91 = f32[8,3,1024]{2,0,1:T(8,128)S(1)} fusion(f32[3,1024,256]{2,1,0:T(8,128)} %get-tuple-element.432, f32[3,1024,256]{2,1,0:T(8,128)S(1)} %get-tuple-element.433, f32[1024,256]{1,0:T(8,128)} %get-tuple-element.434, f32[3,3]{1,0:T(4,128)S(1)} %fusion.90, f32[8,3,1024]{2,0,1:T(8,128)S(1)} %get-tuple-element.472, pred[]{:T(512)S(6)} %compare.15, ...), kind=kOutput, calls=%fused_computation.37.clone.1 | convolution fusion | flops 233619456 | bytes 7563269 | tf_op jit(solution)/shard_map/while/body/eval_jaxpr/abts,kbs->kat/dot_general | solution.py:61
  791.3 2.0 multiply_select_fusion.5
  793.3 2.1 subtract_multiply_fusion.5
  795.5 10.5 %fusion.91 = f32[8,3,1024]{2,0,1:T(8,128)S(1)} fusion(f32[3,1024,256]{2,1,0:T(8,128)} %get-tuple-element.432, f32[3,1024,256]{2,1,0:T(8,128)S(1)} %get-tuple-element.433, f32[1024,256]{1,0:T(8,128)} %get-tuple-element.434, f32[3,3]{1,0:T(4,128)S(1)} %fusion.90, f32[8,3,1024]{2,0,1:T(8,128)S(1)} %get-tuple-element.472, pred[]{:T(512)S(6)} %compare.15, ...), kind=kOutput, calls=%fused_computation.37.clone.1 | convolution fusion | flops 233619456 | bytes 7563269 | tf_op jit(solution)/shard_map/while/body/eval_jaxpr/abts,kbs->kat/dot_general | solution.py:61
  806.4 2.0 multiply_select_fusion.5
  808.4 2.1 subtract_multiply_fusion.5
  810.6 10.5 %fusion.91 = f32[8,3,1024]{2,0,1:T(8,128)S(1)} fusion(f32[3,1024,256]{2,1,0:T(8,128)} %get-tuple-element.432, f32[3,1024,256]{2,1,0:T(8,128)S(1)} %get-tuple-element.433, f32[1024,256]{1,0:T(8,128)} %get-tuple-element.434, f32[3,3]{1,0:T(4,128)S(1)} %fusion.90, f32[8,3,1024]{2,0,1:T(8,128)S(1)} %get-tuple-element.472, pred[]{:T(512)S(6)} %compare.15, ...), kind=kOutput, calls=%fused_computation.37.clone.1 | convolution fusion | flops 233619456 | bytes 7563269 | tf_op jit(solution)/shard_map/while/body/eval_jaxpr/abts,kbs->kat/dot_general | solution.py:61
  821.8 105.6 %all-reduce.5.cloned.1.call-done = f32[8,3,1024]{2,0,1:T(8,128)} async-done(((f32[8,3,1024]{2,0,1:T(8,128)}), f32[8,3,1024]{2,0,1:T(8,128)}) %all-reduce.5.cloned.1.call-update) | async-done | bytes 98320 | tf_op jit(solution)/shard_map/psum | solution.py:66
  927.4 1.6 convolution_subtract_fusion.1
  929.1 104.0 %psum.47 = f32[8,8]{0,1:T(8,128)S(1)} all-reduce(f32[8,8]{0,1:T(8,128)S(1)} %convolution_bitcast_fusion), channel_id=1, replica_groups=mesh['row'=16,'col'=32] {'row','col'}, use_global_device_ids=true, to_apply=%region_13.16 | all-reduce | flops 64 | bytes 512 | tf_op jit(solution)/shard_map/psum | solution.py:79
  (98 shorter events, 18.7 us)
Async XLA Ops:
  7.2 56.4 %copy-start = (f32[8,3,64]{2,0,1:T(8,128)S(1)}, f32[8,3,64]{2,0,1:T(8,128)}, u32[]{:S(2)}) copy-start(f32[8,3,64]{2,0,1:T(8,128)} %param.10) | copy-start | bytes 18436
  7.2 436.9 %all-reduce.3.cloned.1.call-start = ((), (), s32[]{:S(2)}) async-start(), calls=%async_computation | async-start | bytes 196608 | tf_op jit(solution)/shard_map/psum | solution.py:66
  339.8 0.6 copy-start.3
  340.5 586.9 %all-reduce.5.cloned.1.call-start = ((), (), s32[]{:S(2)}) async-start(), calls=%async_computation.1 | async-start | bytes 196608 | tf_op jit(solution)/shard_map/psum | solution.py:66
  653.4 379.7 %copy-start.1 = (f32[8,3,64]{2,0,1:T(8,128)}, f32[8,3,64]{2,0,1:T(8,128)S(1)}, u32[]{:S(2)}) copy-start(f32[8,3,64]{2,0,1:T(8,128)S(1)} %fusion.61) | copy-start | bytes 18436
  821.0 0.6 copy-start.2
Sparse Core Ops, SparseCore 0:
  340.6 103.3 all-reduce.2
  821.8 105.5 all-reduce.4
where the time goes:
time: 1040 us
  blocking collectives  556 us (53%)
  waiting for transfers between devices  209 us (20%)
  matrix products  173 us (17%)
  other arithmetic  80.1 us (8%)
  between operations  14.1 us (1%)
    psum x2, waiting for transfers between devices, mobility(): summed = lax.psum(partial_image, 'row')  209 us
    dot_general x16, matrix products, add_block(): jnp.einsum('abts,kbs->kat', tensor, block_vectors, precision=lax.Precisio...  168 us
    psum x1, blocking collectives, local(): lax.psum(local_gram(noise, noise), ('row', 'col')) / total_count  104 us
    psum x1, blocking collectives, local(): alpha_one = lax.psum(local_gram(first, image), ('row', 'col')) / total_count  104 us
    psum x1, blocking collectives, local(): alpha_two = lax.psum(local_gram(basis, image), ('row', 'col')) / total_count  104 us
    psum x1, blocking collectives, local(): lax.psum(local_gram(remainder, remainder), ('row', 'col')) / total_count  100 us
    all_gather x2, blocking collectives, mobility(): source_piece = lax.all_gather(vectors, 'col', axis=2, tiled=True)  87.6 us
    all_gather x1, blocking collectives, local(): source_pos = lax.all_gather(positions, 'col', axis=1, tiled=True)  38 us
  transfers between devices with their start and end apart: 2, of which 2 were waited for; matrix products, arithmetic and copies ran while one was open for 0% of the time, Pallas kernels for 0%

commit v1 on v0

--- a/solution.py
+++ b/solution.py
@@ -2,6 +2,11 @@
 import jax.numpy as jnp
 from jax import lax
 from jax.sharding import PartitionSpec as P
+
+
+def axis_by_axis(array, axis_one, axis_two):
+    half = lax.psum(array, axis_one)
+    return lax.psum(half, axis_two)
 
 
 def pair_tensor(target_pos, source_pos):
@@ -66,7 +71,7 @@
         summed = lax.psum(partial_image, "row")
         return lax.dynamic_slice_in_dim(summed, lax.axis_index("row") * local_beads, local_beads, 2)
 
-    start_matrix = lax.psum(local_gram(noise, noise), ("row", "col")) / total_count
+    start_matrix = axis_by_axis(local_gram(noise, noise), "row", "col") / total_count
     start_factor = jnp.linalg.cholesky(start_matrix)
     first = combine(noise, lower_inverse(start_factor).T)
     image = mobility(first)

time: 1040 us -> 1030 us (level)
  blocking collectives: 556 us -> 541 us
    psum x1 -> x2, blocking collectives: 104 us -> 88.8 us  [the longest x1 57.9 us: axis_by_axis(): return lax.psum(half, axis_two)]
where the time goes in v1:
time: 1030 us; the launch traced here: 1020 us
  blocking collectives  541 us (53%)
  waiting for transfers between devices  208 us (20%)
  matrix products  173 us (17%)
  other arithmetic  80.1 us (8%)
  between operations  14.1 us (1%)
    psum x2, waiting for transfers between devices, mobility(): summed = lax.psum(partial_image, 'row')  208 us
    dot_general x16, matrix products, add_block(): jnp.einsum('abts,kbs->kat', tensor, block_vectors, precision=lax.Precisio...  168 us
    psum x1, blocking collectives, local(): alpha_one = lax.psum(local_gram(first, image), ('row', 'col')) / total_count  104 us
    psum x1, blocking collectives, local(): alpha_two = lax.psum(local_gram(basis, image), ('row', 'col')) / total_count  104 us
    psum x1, blocking collectives, local(): lax.psum(local_gram(remainder, remainder), ('row', 'col')) / total_count  100 us
    all_gather x2, blocking collectives, mobility(): source_piece = lax.all_gather(vectors, 'col', axis=2, tiled=True)  87.1 us
    psum x1, blocking collectives, axis_by_axis(): return lax.psum(half, axis_two)  57.9 us
    all_gather x1, blocking collectives, local(): source_pos = lax.all_gather(positions, 'col', axis=1, tiled=True)  38 us
  transfers between devices with their start and end apart: 2, of which 2 were waited for; matrix products, arithmetic and copies ran while one was open for 0% of the time, Pallas kernels for 0%

profile of v1, /device:TPU:1, one launch (start us, length us, event | category | flops | bytes accessed | tf_op | source)
XLA Modules:
  0.0 1024.4 jit_solution(16390685396233314855)
XLA Ops:
  7.2 38.0 %all-gather.1 = f32[32,64,3]{1,2,0:T(4,128)S(1)} all-gather(f32[1,64,3]{1,2,0:T(4,128)} %bitcast.96), channel_id=1, replica_groups=mesh['row'=16,'col'=32] {'col'}, dimensions={0}, use_global_device_ids=true | all-gather | bytes 25344 | tf_op jit(solution)/shard_map/all_gather | solution.py:47
  45.2 18.3 %all-gather = f32[16,64,3]{1,2,0:T(4,128)S(1)} all-gather(f32[1,64,3]{1,2,0:T(4,128)} %bitcast.97), channel_id=1, replica_groups=mesh['row'=16,'col'=32] {'row'}, dimensions={0}, use_global_device_ids=true | all-gather | bytes 13056 | tf_op jit(solution)/shard_map/all_gather | solution.py:46
  63.7 30.9 %psum.49 = f32[8,8]{0,1:T(8,128)S(1)} all-reduce(f32[8,8]{0,1:T(8,128)S(1)} %convolution_bitcast_fusion.5), channel_id=1, replica_groups=mesh['row'=16,'col'=32] {'row'}, use_global_device_ids=true, to_apply=%region_0.0 | all-reduce | flops 64 | bytes 512 | tf_op jit(solution)/shard_map/psum | solution.py:8
  94.6 57.9 %psum.50 = f32[8,8]{0,1:T(8,128)S(1)} all-reduce(f32[8,8]{0,1:T(8,128)S(1)} %psum.49), channel_id=1, replica_groups=mesh['row'=16,'col'=32] {'col'}, use_global_device_ids=true, to_apply=%region_1.0 | all-reduce | flops 64 | bytes 512 | tf_op jit(solution)/shard_map/psum | solution.py:9
  155.7 43.8 %all_gather.12 = f32[8,3,2048]{0,1,2:T(4,128)} all-gather(f32[8,3,64]{0,1,2:T(4,128)S(1)} %copy.36), channel_id=1, replica_groups=mesh['row'=16,'col'=32] {'col'}, dimensions={2}, use_global_device_ids=true | all-gather | bytes 202752 | tf_op jit(solution)/shard_map/all_gather | solution.py:51
  199.5 3.3 copy.39
  203.0 120.9 %while.32 = (s32[]{:T(128)}, f32[8,3,1024]{2,0,1:T(8,128)S(1)}, f32[8,3,2048]{2,0,1:T(8,128)S(1)}, f32[3,1024]{1,0:T(4,128)S(1)}, f32[3,2048]{1,0:T(4,128)S(1)},...) while((s32[]{:T(128)}, f32[8,3,1024]{2,0,1:T(8,128)S(1)}, f32[8,3,2048]{2,0,1:T(8,128)S(1)}, ...), condition=%wide.region_6.9_spmd.clone, body=%wide.region_4.8_spmd.clone.sunk | while | flops 242270240 | bytes 19134656 | solution.py:70
  203.5 2.0 multiply_select_fusion.4
  205.5 2.1 subtract_multiply_fusion.4
  207.7 10.5 %fusion.87 = f32[8,3,1024]{2,0,1:T(8,128)S(1)} fusion(f32[3,1024,256]{2,1,0:T(8,128)} %get-tuple-element.423, f32[3,1024,256]{2,1,0:T(8,128)S(1)} %get-tuple-element.424, f32[1024,256]{1,0:T(8,128)} %get-tuple-element.425, f32[3,3]{1,0:T(4,128)S(1)} %fusion.86, f32[8,3,1024]{2,0,1:T(8,128)S(1)} %get-tuple-element.445, pred[]{:T(512)S(6)} %compare.14, ...), kind=kOutput, calls=%fused_computation.13.clone.1 | convolution fusion | flops 233619456 | bytes 7563269 | tf_op jit(solution)/shard_map/while/body/eval_jaxpr/abts,kbs->kat/dot_general | solution.py:66
  218.6 2.0 multiply_select_fusion.4
  220.6 2.1 subtract_multiply_fusion.4
  222.8 10.5 %fusion.87 = f32[8,3,1024]{2,0,1:T(8,128)S(1)} fusion(f32[3,1024,256]{2,1,0:T(8,128)} %get-tuple-element.423, f32[3,1024,256]{2,1,0:T(8,128)S(1)} %get-tuple-element.424, f32[1024,256]{1,0:T(8,128)} %get-tuple-element.425, f32[3,3]{1,0:T(4,128)S(1)} %fusion.86, f32[8,3,1024]{2,0,1:T(8,128)S(1)} %get-tuple-element.445, pred[]{:T(512)S(6)} %compare.14, ...), kind=kOutput, calls=%fused_computation.13.clone.1 | convolution fusion | flops 233619456 | bytes 7563269 | tf_op jit(solution)/shard_map/while/body/eval_jaxpr/abts,kbs->kat/dot_general | solution.py:66
  233.8 2.0 multiply_select_fusion.4
  235.8 2.1 subtract_multiply_fusion.4
  237.9 10.5 %fusion.87 = f32[8,3,1024]{2,0,1:T(8,128)S(1)} fusion(f32[3,1024,256]{2,1,0:T(8,128)} %get-tuple-element.423, f32[3,1024,256]{2,1,0:T(8,128)S(1)} %get-tuple-element.424, f32[1024,256]{1,0:T(8,128)} %get-tuple-element.425, f32[3,3]{1,0:T(4,128)S(1)} %fusion.86, f32[8,3,1024]{2,0,1:T(8,128)S(1)} %get-tuple-element.445, pred[]{:T(512)S(6)} %compare.14, ...), kind=kOutput, calls=%fused_computation.13.clone.1 | convolution fusion | flops 233619456 | bytes 7563269 | tf_op jit(solution)/shard_map/while/body/eval_jaxpr/abts,kbs->kat/dot_general | solution.py:66
  248.9 2.0 multiply_select_fusion.4
  250.9 2.1 subtract_multiply_fusion.4
  253.0 10.5 %fusion.87 = f32[8,3,1024]{2,0,1:T(8,128)S(1)} fusion(f32[3,1024,256]{2,1,0:T(8,128)} %get-tuple-element.423, f32[3,1024,256]{2,1,0:T(8,128)S(1)} %get-tuple-element.424, f32[1024,256]{1,0:T(8,128)} %get-tuple-element.425, f32[3,3]{1,0:T(4,128)S(1)} %fusion.86, f32[8,3,1024]{2,0,1:T(8,128)S(1)} %get-tuple-element.445, pred[]{:T(512)S(6)} %compare.14, ...), kind=kOutput, calls=%fused_computation.13.clone.1 | convolution fusion | flops 233619456 | bytes 7563269 | tf_op jit(solution)/shard_map/while/body/eval_jaxpr/abts,kbs->kat/dot_general | solution.py:66
  264.0 2.0 multiply_select_fusion.4
  266.0 2.1 subtract_multiply_fusion.4
  268.1 10.5 %fusion.87 = f32[8,3,1024]{2,0,1:T(8,128)S(1)} fusion(f32[3,1024,256]{2,1,0:T(8,128)} %get-tuple-element.423, f32[3,1024,256]{2,1,0:T(8,128)S(1)} %get-tuple-element.424, f32[1024,256]{1,0:T(8,128)} %get-tuple-element.425, f32[3,3]{1,0:T(4,128)S(1)} %fusion.86, f32[8,3,1024]{2,0,1:T(8,128)S(1)} %get-tuple-element.445, pred[]{:T(512)S(6)} %compare.14, ...), kind=kOutput, calls=%fused_computation.13.clone.1 | convolution fusion | flops 233619456 | bytes 7563269 | tf_op jit(solution)/shard_map/while/body/eval_jaxpr/abts,kbs->kat/dot_general | solution.py:66
  279.1 2.0 multiply_select_fusion.4
  281.1 2.1 subtract_multiply_fusion.4
  283.2 10.5 %fusion.87 = f32[8,3,1024]{2,0,1:T(8,128)S(1)} fusion(f32[3,1024,256]{2,1,0:T(8,128)} %get-tuple-element.423, f32[3,1024,256]{2,1,0:T(8,128)S(1)} %get-tuple-element.424, f32[1024,256]{1,0:T(8,128)} %get-tuple-element.425, f32[3,3]{1,0:T(4,128)S(1)} %fusion.86, f32[8,3,1024]{2,0,1:T(8,128)S(1)} %get-tuple-element.445, pred[]{:T(512)S(6)} %compare.14, ...), kind=kOutput, calls=%fused_computation.13.clone.1 | convolution fusion | flops 233619456 | bytes 7563269 | tf_op jit(solution)/shard_map/while/body/eval_jaxpr/abts,kbs->kat/dot_general | solution.py:66
  294.2 2.0 multiply_select_fusion.4
  296.2 2.1 subtract_multiply_fusion.4
  298.4 10.5 %fusion.87 = f32[8,3,1024]{2,0,1:T(8,128)S(1)} fusion(f32[3,1024,256]{2,1,0:T(8,128)} %get-tuple-element.423, f32[3,1024,256]{2,1,0:T(8,128)S(1)} %get-tuple-element.424, f32[1024,256]{1,0:T(8,128)} %get-tuple-element.425, f32[3,3]{1,0:T(4,128)S(1)} %fusion.86, f32[8,3,1024]{2,0,1:T(8,128)S(1)} %get-tuple-element.445, pred[]{:T(512)S(6)} %compare.14, ...), kind=kOutput, calls=%fused_computation.13.clone.1 | convolution fusion | flops 233619456 | bytes 7563269 | tf_op jit(solution)/shard_map/while/body/eval_jaxpr/abts,kbs->kat/dot_general | solution.py:66
  309.3 2.0 multiply_select_fusion.4
  311.3 2.1 subtract_multiply_fusion.4
  313.5 10.5 %fusion.87 = f32[8,3,1024]{2,0,1:T(8,128)S(1)} fusion(f32[3,1024,256]{2,1,0:T(8,128)} %get-tuple-element.423, f32[3,1024,256]{2,1,0:T(8,128)S(1)} %get-tuple-element.424, f32[1024,256]{1,0:T(8,128)} %get-tuple-element.425, f32[3,3]{1,0:T(4,128)S(1)} %fusion.86, f32[8,3,1024]{2,0,1:T(8,128)S(1)} %get-tuple-element.445, pred[]{:T(512)S(6)} %compare.14, ...), kind=kOutput, calls=%fused_computation.13.clone.1 | convolution fusion | flops 233619456 | bytes 7563269 | tf_op jit(solution)/shard_map/while/body/eval_jaxpr/abts,kbs->kat/dot_general | solution.py:66
  324.7 102.4 %all-reduce.3.cloned.1.call-done = f32[8,3,1024]{2,0,1:T(8,128)} async-done(((f32[8,3,1024]{2,0,1:T(8,128)}), f32[8,3,1024]{2,0,1:T(8,128)}) %all-reduce.3.cloned.1.call-update) | async-done | bytes 98320 | tf_op jit(solution)/shard_map/psum | solution.py:71
  428.0 104.0 %psum.52 = f32[8,8]{0,1:T(8,128)S(1)} all-reduce(f32[8,8]{0,1:T(8,128)S(1)} %convolution_bitcast_fusion.3), channel_id=1, replica_groups=mesh['row'=16,'col'=32] {'row','col'}, use_global_device_ids=true, to_apply=%region_8.11 | all-reduce | flops 64 | bytes 512 | tf_op jit(solution)/shard_map/psum | solution.py:78
  532.9 100.4 %psum.53 = f32[8,8]{0,1:T(8,128)S(1)} all-reduce(f32[8,8]{0,1:T(8,128)S(1)} %convolution_bitcast_fusion.2), channel_id=1, replica_groups=mesh['row'=16,'col'=32] {'row','col'}, use_global_device_ids=true, to_apply=%region_9.12 | all-reduce | flops 64 | bytes 512 | tf_op jit(solution)/shard_map/psum | solution.py:80
  636.6 43.3 %all_gather.15 = f32[8,3,2048]{0,1,2:T(4,128)} all-gather(f32[8,3,64]{0,1,2:T(4,128)S(1)} %copy.44), channel_id=1, replica_groups=mesh['row'=16,'col'=32] {'col'}, dimensions={2}, use_global_device_ids=true | all-gather | bytes 202752 | tf_op jit(solution)/shard_map/all_gather | solution.py:51
  679.9 3.3 copy.45
  683.2 120.9 %while.33 = (s32[]{:T(128)}, f32[8,3,1024]{2,0,1:T(8,128)S(1)}, f32[8,3,2048]{2,0,1:T(8,128)S(1)}, f32[3,1024]{1,0:T(4,128)S(1)}, f32[3,2048]{1,0:T(4,128)S(1)},...) while((s32[]{:T(128)}, f32[8,3,1024]{2,0,1:T(8,128)S(1)}, f32[8,3,2048]{2,0,1:T(8,128)S(1)}, ...), condition=%wide.region_12.15_spmd.clone, body=%wide.region_10.14_spmd.clone.sunk | while | flops 242270240 | bytes 19134656 | solution.py:70
  683.7 2.0 multiply_select_fusion.5
  685.7 2.1 subtract_multiply_fusion.5
  687.8 10.5 %fusion.91 = f32[8,3,1024]{2,0,1:T(8,128)S(1)} fusion(f32[3,1024,256]{2,1,0:T(8,128)} %get-tuple-element.432, f32[3,1024,256]{2,1,0:T(8,128)S(1)} %get-tuple-element.433, f32[1024,256]{1,0:T(8,128)} %get-tuple-element.434, f32[3,3]{1,0:T(4,128)S(1)} %fusion.90, f32[8,3,1024]{2,0,1:T(8,128)S(1)} %get-tuple-element.472, pred[]{:T(512)S(6)} %compare.15, ...), kind=kOutput, calls=%fused_computation.37.clone.1 | convolution fusion | flops 233619456 | bytes 7563269 | tf_op jit(solution)/shard_map/while/body/eval_jaxpr/abts,kbs->kat/dot_general | solution.py:66
  698.8 2.0 multiply_select_fusion.5
  700.8 2.1 subtract_multiply_fusion.5
  702.9 10.5 %fusion.91 = f32[8,3,1024]{2,0,1:T(8,128)S(1)} fusion(f32[3,1024,256]{2,1,0:T(8,128)} %get-tuple-element.432, f32[3,1024,256]{2,1,0:T(8,128)S(1)} %get-tuple-element.433, f32[1024,256]{1,0:T(8,128)} %get-tuple-element.434, f32[3,3]{1,0:T(4,128)S(1)} %fusion.90, f32[8,3,1024]{2,0,1:T(8,128)S(1)} %get-tuple-element.472, pred[]{:T(512)S(6)} %compare.15, ...), kind=kOutput, calls=%fused_computation.37.clone.1 | convolution fusion | flops 233619456 | bytes 7563269 | tf_op jit(solution)/shard_map/while/body/eval_jaxpr/abts,kbs->kat/dot_general | solution.py:66
  713.9 2.0 multiply_select_fusion.5
  715.9 2.1 subtract_multiply_fusion.5
  718.1 10.5 %fusion.91 = f32[8,3,1024]{2,0,1:T(8,128)S(1)} fusion(f32[3,1024,256]{2,1,0:T(8,128)} %get-tuple-element.432, f32[3,1024,256]{2,1,0:T(8,128)S(1)} %get-tuple-element.433, f32[1024,256]{1,0:T(8,128)} %get-tuple-element.434, f32[3,3]{1,0:T(4,128)S(1)} %fusion.90, f32[8,3,1024]{2,0,1:T(8,128)S(1)} %get-tuple-element.472, pred[]{:T(512)S(6)} %compare.15, ...), kind=kOutput, calls=%fused_computation.37.clone.1 | convolution fusion | flops 233619456 | bytes 7563269 | tf_op jit(solution)/shard_map/while/body/eval_jaxpr/abts,kbs->kat/dot_general | solution.py:66
  729.0 2.0 multiply_select_fusion.5
  731.0 2.1 subtract_multiply_fusion.5
  733.2 10.5 %fusion.91 = f32[8,3,1024]{2,0,1:T(8,128)S(1)} fusion(f32[3,1024,256]{2,1,0:T(8,128)} %get-tuple-element.432, f32[3,1024,256]{2,1,0:T(8,128)S(1)} %get-tuple-element.433, f32[1024,256]{1,0:T(8,128)} %get-tuple-element.434, f32[3,3]{1,0:T(4,128)S(1)} %fusion.90, f32[8,3,1024]{2,0,1:T(8,128)S(1)} %get-tuple-element.472, pred[]{:T(512)S(6)} %compare.15, ...), kind=kOutput, calls=%fused_computation.37.clone.1 | convolution fusion | flops 233619456 | bytes 7563269 | tf_op jit(solution)/shard_map/while/body/eval_jaxpr/abts,kbs->kat/dot_general | solution.py:66
  744.1 2.0 multiply_select_fusion.5
  746.1 2.1 subtract_multiply_fusion.5
  748.3 10.5 %fusion.91 = f32[8,3,1024]{2,0,1:T(8,128)S(1)} fusion(f32[3,1024,256]{2,1,0:T(8,128)} %get-tuple-element.432, f32[3,1024,256]{2,1,0:T(8,128)S(1)} %get-tuple-element.433, f32[1024,256]{1,0:T(8,128)} %get-tuple-element.434, f32[3,3]{1,0:T(4,128)S(1)} %fusion.90, f32[8,3,1024]{2,0,1:T(8,128)S(1)} %get-tuple-element.472, pred[]{:T(512)S(6)} %compare.15, ...), kind=kOutput, calls=%fused_computation.37.clone.1 | convolution fusion | flops 233619456 | bytes 7563269 | tf_op jit(solution)/shard_map/while/body/eval_jaxpr/abts,kbs->kat/dot_general | solution.py:66
  759.3 2.0 multiply_select_fusion.5
  761.3 2.1 subtract_multiply_fusion.5
  763.4 10.5 %fusion.91 = f32[8,3,1024]{2,0,1:T(8,128)S(1)} fusion(f32[3,1024,256]{2,1,0:T(8,128)} %get-tuple-element.432, f32[3,1024,256]{2,1,0:T(8,128)S(1)} %get-tuple-element.433, f32[1024,256]{1,0:T(8,128)} %get-tuple-element.434, f32[3,3]{1,0:T(4,128)S(1)} %fusion.90, f32[8,3,1024]{2,0,1:T(8,128)S(1)} %get-tuple-element.472, pred[]{:T(512)S(6)} %compare.15, ...), kind=kOutput, calls=%fused_computation.37.clone.1 | convolution fusion | flops 233619456 | bytes 7563269 | tf_op jit(solution)/shard_map/while/body/eval_jaxpr/abts,kbs->kat/dot_general | solution.py:66
  774.4 2.0 multiply_select_fusion.5
  776.4 2.1 subtract_multiply_fusion.5
  778.5 10.5 %fusion.91 = f32[8,3,1024]{2,0,1:T(8,128)S(1)} fusion(f32[3,1024,256]{2,1,0:T(8,128)} %get-tuple-element.432, f32[3,1024,256]{2,1,0:T(8,128)S(1)} %get-tuple-element.433, f32[1024,256]{1,0:T(8,128)} %get-tuple-element.434, f32[3,3]{1,0:T(4,128)S(1)} %fusion.90, f32[8,3,1024]{2,0,1:T(8,128)S(1)} %get-tuple-element.472, pred[]{:T(512)S(6)} %compare.15, ...), kind=kOutput, calls=%fused_computation.37.clone.1 | convolution fusion | flops 233619456 | bytes 7563269 | tf_op jit(solution)/shard_map/while/body/eval_jaxpr/abts,kbs->kat/dot_general | solution.py:66
  789.5 2.0 multiply_select_fusion.5
  791.5 2.1 subtract_multiply_fusion.5
  793.6 10.5 %fusion.91 = f32[8,3,1024]{2,0,1:T(8,128)S(1)} fusion(f32[3,1024,256]{2,1,0:T(8,128)} %get-tuple-element.432, f32[3,1024,256]{2,1,0:T(8,128)S(1)} %get-tuple-element.433, f32[1024,256]{1,0:T(8,128)} %get-tuple-element.434, f32[3,3]{1,0:T(4,128)S(1)} %fusion.90, f32[8,3,1024]{2,0,1:T(8,128)S(1)} %get-tuple-element.472, pred[]{:T(512)S(6)} %compare.15, ...), kind=kOutput, calls=%fused_computation.37.clone.1 | convolution fusion | flops 233619456 | bytes 7563269 | tf_op jit(solution)/shard_map/while/body/eval_jaxpr/abts,kbs->kat/dot_general | solution.py:66
  804.8 105.6 %all-reduce.5.cloned.1.call-done = f32[8,3,1024]{2,0,1:T(8,128)} async-done(((f32[8,3,1024]{2,0,1:T(8,128)}), f32[8,3,1024]{2,0,1:T(8,128)}) %all-reduce.5.cloned.1.call-update) | async-done | bytes 98320 | tf_op jit(solution)/shard_map/psum | solution.py:71
  910.5 1.6 convolution_subtract_fusion.1
  912.2 104.0 %psum.55 = f32[8,8]{0,1:T(8,128)S(1)} all-reduce(f32[8,8]{0,1:T(8,128)S(1)} %convolution_bitcast_fusion), channel_id=1, replica_groups=mesh['row'=16,'col'=32] {'row','col'}, use_global_device_ids=true, to_apply=%region_14.17 | all-reduce | flops 64 | bytes 512 | tf_op jit(solution)/shard_map/psum | solution.py:84
  (99 shorter events, 19.6 us)
Async XLA Ops:
  7.2 56.4 %copy-start = (f32[8,3,64]{2,0,1:T(8,128)S(1)}, f32[8,3,64]{2,0,1:T(8,128)}, u32[]{:S(2)}) copy-start(f32[8,3,64]{2,0,1:T(8,128)} %param.10) | copy-start | bytes 18436
  7.2 419.9 %all-reduce.3.cloned.1.call-start = ((), (), s32[]{:S(2)}) async-start(), calls=%async_computation | async-start | bytes 196608 | tf_op jit(solution)/shard_map/psum | solution.py:71
  323.9 0.6 copy-start.3
  324.6 585.8 %all-reduce.5.cloned.1.call-start = ((), (), s32[]{:S(2)}) async-start(), calls=%async_computation.1 | async-start | bytes 196608 | tf_op jit(solution)/shard_map/psum | solution.py:71
  636.4 379.7 %copy-start.1 = (f32[8,3,64]{2,0,1:T(8,128)}, f32[8,3,64]{2,0,1:T(8,128)S(1)}, u32[]{:S(2)}) copy-start(f32[8,3,64]{2,0,1:T(8,128)S(1)} %fusion.61) | copy-start | bytes 18436
  804.1 0.6 copy-start.2
Sparse Core Ops, SparseCore 0:
  324.7 102.2 all-reduce.2
  804.9 105.5 all-reduce.4
